TPU v7x, 128 devices: a whole 4x4x4 slice. The times are simulated.
128 devices in a mesh: band: 8 (over x, core), col: 16 (over y, z).
Axes of the slice: x: 4, y: 4, z: 4, core: 2. Of those that a mesh axis runs over, the one named last changes fastest.
Arguments:
- series: float32 [16, 32768], P(None, ('band', 'col')), may hold values from -6 to 6
- tail: float32 [16, 255], replicated, may hold values from -6 to 6
Outputs:
- profile: float32 [16, 32768], P(None, ('band', 'col'))
All inputs are finite; a program needn't handle non-finite values.
Results may differ from a plain program's by a relative error of at most 0.0003.
Values may be sent and summed in bfloat16 or wider, within the bound.
No kernel may reach another device: no remote copies, remote signals or barrier semaphores. Data moves between devices by JAX's collectives and lax.ppermute only.
A program may use at most 64 MiB of HBM per device.

v0:
```python
import functools

import jax
import jax.numpy as jnp
from jax import lax
from jax.experimental import pallas as pl
from jax.experimental.pallas import tpu as pltpu
from jax.sharding import PartitionSpec as P

AXES = ("band", "col")
KD = 4
EPSILON = 1e-06
ROW = 4
BLOCK = 256
LANES = 128
HALO = KD - 1
SPAN = 2 * HALO + 1


def permute(block, target, count):
    return lax.ppermute(block, AXES, [(i, target(i) % count) for i in range(count)])


def shifted(block, by):
    return pltpu.roll(block, block.shape[1] - by, 1)


def kernel(row_ref, after_ref, before_ref, tail_ref, out_ref, line, wave, mean, scale, z_ref, best_ref):
    channels = out_ref.shape[0]
    place = lax.axis_index("band") * lax.axis_size("col") + lax.axis_index("col")
    count = lax.axis_size("band") * lax.axis_size("col")
    here = lax.rem(place, ROW)

    for piece in range(ROW):
        at = (here ^ piece) * BLOCK
        source = slice(piece * BLOCK, (piece + 1) * BLOCK)
        for turn, ref in enumerate((before_ref, row_ref, after_ref)):
            target = pl.multiple_of(at + turn * ROW * BLOCK, BLOCK)
            line[:, pl.ds(target, BLOCK)] = ref[:, source]

    @pl.when(place + ROW >= count)
    def _():
        line[:, 2 * ROW * BLOCK : 2 * ROW * BLOCK + BLOCK] = tail_ref[...]

    start = pl.multiple_of((here + ROW - HALO) * BLOCK, BLOCK)
    x = line[:, pl.ds(start, (SPAN + 1) * BLOCK)]
    for l in range((SPAN + 1) * 2):
        wave[l] = x[:, l * LANES : (l + 1) * LANES]

    average, spread = x, jnp.zeros_like(x)
    width = 1
    while width < BLOCK:
        other = shifted(average, width)
        gap = other - average
        spread = spread + shifted(spread, width) + gap * gap * (0.5 * width)
        average = average + 0.5 * gap
        width *= 2
    spread = lax.rsqrt(spread * (1.0 / BLOCK) + EPSILON)
    for l in range(SPAN * 2):
        mean[l] = average[:, l * LANES : (l + 1) * LANES]
        scale[l] = spread[:, l * LANES : (l + 1) * LANES]

    low = lax.broadcasted_iota(jnp.int32, (LANES, LANES), 1)
    low = low <= lax.broadcasted_iota(jnp.int32, (LANES, LANES), 0)
    lag = lax.broadcasted_iota(jnp.int32, (BLOCK, BLOCK), 1)
    lag = lag - lax.broadcasted_iota(jnp.int32, (BLOCK, BLOCK), 0)

    def line_of(ref, c, l):
        row = ref[l, pl.ds(c, 8, stride=0), :]
        return jnp.broadcast_to(row[None], (LANES // 8, 8, LANES)).reshape(LANES, LANES)

    def turned(c, l):
        return pltpu.roll(line_of(wave, c, l), 1, 1, stride=1, stride_axis=0)

    def channel(c, carry):
        first = turned(c, 0)
        second = turned(c, 1)
        near = jnp.where(low, first, second)
        for l in range(SPAN * 2):
            third = turned(c, l + 2)
            far = jnp.where(low, second, third)
            at = slice(l * LANES, (l + 1) * LANES)
            a = line_of(mean, c, l)
            r = line_of(scale, c, l)
            z_ref[:LANES, at] = ((near - a) * r).astype(jnp.bfloat16)
            z_ref[LANES:, at] = ((far - a) * r).astype(jnp.bfloat16)
            near, second = far, third
        own = z_ref[:, HALO * BLOCK : (HALO + 1) * BLOCK].T
        best = jnp.full((BLOCK, LANES), -4.0, jnp.float32)
        for b in range(SPAN):
            score = jnp.dot(own, z_ref[:, b * BLOCK : (b + 1) * BLOCK], preferred_element_type=jnp.float32) * (1.0 / BLOCK)
            offset = b - HALO
            if abs(offset) <= 1:
                score = jnp.where(jnp.abs(lag + offset * BLOCK) >= BLOCK // 4, score, -4.0)
            top = jnp.maximum(score[:, :LANES], score[:, LANES:])
            if offset:
                valid = (place + offset >= 0) & (place + offset < count)
                top = jnp.where(valid, top, -4.0)
            best = jnp.maximum(best, top)
        best_ref[pl.ds(c, 1), :] = jnp.max(best.T, axis=0, keepdims=True)
        return carry

    lax.fori_loop(0, channels, channel, 0)
    out_ref[...] = jnp.sqrt(2.0 * BLOCK * (1.0 - best_ref[...]))


def shards(series, tail):
    channels = series.shape[0]
    count = lax.axis_size(AXES)
    tail = jnp.pad(tail, ((0, 0), (0, 1)))
    pair = jnp.concatenate([series, permute(series, lambda i: i ^ 1, count)], axis=1)
    row = jnp.concatenate([pair, permute(pair, lambda i: i ^ 2, count)], axis=1)
    after = permute(row, lambda i: i - ROW, count)
    before = permute(row, lambda i: i + ROW, count)
    vmem = pl.BlockSpec(memory_space=pltpu.VMEM)
    return pl.pallas_call(
        kernel,
        out_shape=jax.ShapeDtypeStruct((channels, BLOCK), jnp.float32),
        in_specs=[vmem] * 4,
        out_specs=vmem,
        scratch_shapes=[
            pltpu.VMEM((channels, 3 * ROW * BLOCK), jnp.float32),
            pltpu.VMEM(((SPAN + 1) * 2, channels, LANES), jnp.float32),
            pltpu.VMEM((SPAN * 2, channels, LANES), jnp.float32),
            pltpu.VMEM((SPAN * 2, channels, LANES), jnp.float32),
            pltpu.VMEM((BLOCK, SPAN * BLOCK), jnp.bfloat16),
            pltpu.VMEM((channels, BLOCK), jnp.float32),
        ],
    )(row, after, before, tail)


def solution(mesh):
    return jax.shard_map(
        shards,
        mesh=mesh,
        in_specs=(P(None, AXES), P()),
        out_specs=P(None, AXES),
        check_vma=False,
    )
```

profile of v0, /device:TPU:0, one launch (start us, length us, event | category | flops | bytes accessed | tf_op | source)
XLA Modules:
  0.0 32.6 jit_solution(4543135565744324884)
XLA Ops:
  0.0 0.0 copy-start.3
  0.0 2.0 %collective-permute-start = (f32[16,256]{1,0:T(8,128)}, f32[16,256]{1,0:T(8,128)S(1)}, u32[]{:S(2)}, u32[]{:S(2)}) collective-permute-start(f32[16,256]{1,0:T(8,128)} %param.2), channel_id=1, source_target_pairs={{0,1},{1,0},{2,3},{3,2},{4,5},{5,4},{6,7},{7,6},{8,9},{9,8},{10,11... | collective-permute-start | bytes 49160 | tf_op jit(solution)/shard_map/ppermute | solution.py:21
  2.0 0.8 %constant_dynamic-update-slice_fusion.2 = f32[16,1024]{1,0:T(8,128)S(1)} fusion(f32[16,256]{1,0:T(8,128)} %param.2), kind=kLoop, calls=%fused_computation.3 | loop fusion | bytes 32768
  2.8 1.2 %collective-permute-done = f32[16,256]{1,0:T(8,128)S(1)} collective-permute-done((f32[16,256]{1,0:T(8,128)}, f32[16,256]{1,0:T(8,128)S(1)}, u32[]{:S(2)}, u32[]{:S(2)}) %collective-permute-start) | collective-permute-done | bytes 16416 | tf_op jit(solution)/shard_map/ppermute | solution.py:21
  4.0 0.0 copy-done.3
  4.0 3.9 %collective-permute-start.1 = (f32[16,512]{1,0:T(8,128)S(1)}, f32[16,512]{1,0:T(8,128)S(1)}, u32[]{:S(2)}, u32[]{:S(2)}) collective-permute-start(f32[16,512]{1,0:T(8,128)S(1)} %pad_maximum_fusion), channel_id=1, source_target_pairs={{0,2},{1,3},{2,0},{3,1},{4,6},{5,7},{6,4},{7,5},{8,10},{9,11},{10,... | collective-permute-start | bytes 98312 | tf_op jit(solution)/shard_map/ppermute | solution.py:21
  8.0 0.0 copy-start.4
  8.0 1.9 %collective-permute-done.1 = f32[16,512]{1,0:T(8,128)S(1)} collective-permute-done((f32[16,512]{1,0:T(8,128)S(1)}, f32[16,512]{1,0:T(8,128)S(1)}, u32[]{:S(2)}, u32[]{:S(2)}) %collective-permute-start.1) | collective-permute-done | bytes 32800 | tf_op jit(solution)/shard_map/ppermute | solution.py:21
  9.8 0.0 copy-start
  9.8 1.6 %collective-permute-start.3 = (f32[16,1024]{1,0:T(8,128)S(1)}, f32[16,1024]{1,0:T(8,128)S(1)}, u32[]{:S(2)}, u32[]{:S(2)}) collective-permute-start(f32[16,1024]{1,0:T(8,128)S(1)} %constant_dynamic-update-slice_fusion.row_ref), channel_id=1, source_target_pairs={{0,4},{1,5},{2,6},{3,7},{4,8},{5,9},{6,10},{7,11},{8,12},{9,13},{1... | collective-permute-start | bytes 196616 | tf_op jit(solution)/shard_map/ppermute | solution.py:21
  11.4 3.5 %collective-permute-start.2 = (f32[16,1024]{1,0:T(8,128)S(1)}, f32[16,1024]{1,0:T(8,128)S(1)}, u32[]{:S(2)}, u32[]{:S(2)}) collective-permute-start(f32[16,1024]{1,0:T(8,128)S(1)} %constant_dynamic-update-slice_fusion.row_ref), channel_id=1, source_target_pairs={{0,124},{1,125},{2,126},{3,127},{4,0},{5,1},{6,2},{7,3},{8,4},{9,5... | collective-permute-start | bytes 196616 | tf_op jit(solution)/shard_map/ppermute | solution.py:21
  14.9 0.0 copy-done.4
  14.9 0.6 %pad.4.tail_ref = f32[16,256]{1,0:T(8,128)} pad(f32[16,255]{1,0:T(8,128)S(1)} %copy-done.4, f32[]{:T(128)} %constant.2.clone.1), padding=0_0x0_1 | pad | bytes 32708 | tf_op jit(solution)/shard_map/jit(_pad)/pad | solution.py:110
  15.5 1.3 %collective-permute-done.3.before_ref = f32[16,1024]{1,0:T(8,128)S(1)} collective-permute-done((f32[16,1024]{1,0:T(8,128)S(1)}, f32[16,1024]{1,0:T(8,128)S(1)}, u32[]{:S(2)}, u32[]{:S(2)}) %collective-permute-start.3) | collective-permute-done | bytes 65568 | tf_op jit(solution)/shard_map/ppermute | solution.py:21
  16.9 0.0 copy-start.1
  16.9 0.0 collective-permute-done.2.after_ref
  16.9 0.0 copy-done
  16.9 0.6 %copy-done.1 = f32[16,1024]{1,0:T(8,128)} copy-done((f32[16,1024]{1,0:T(8,128)}, f32[16,1024]{1,0:T(8,128)S(1)}, u32[]{:S(2)}) %copy-start.1) | copy-done | bytes 65560
  17.5 0.0 copy-start.2
  17.5 0.6 %copy-done.2 = f32[16,1024]{1,0:T(8,128)} copy-done((f32[16,1024]{1,0:T(8,128)}, f32[16,1024]{1,0:T(8,128)S(1)}, u32[]{:S(2)}) %copy-start.2) | copy-done | bytes 65560
  18.1 14.5 %shard_map.28 = f32[16,256]{1,0:T(8,128)} custom-call(f32[16,1024]{1,0:T(8,128)} %copy-done, f32[16,1024]{1,0:T(8,128)} %copy-done.2, f32[16,1024]{1,0:T(8,128)} %copy-done.1, f32[16,256]{1,0:T(8,128)} %pad.4.tail_ref), custom_call_target="tpu_custom_call" | custom-call | tf_op jit(solution)/shard_map/pallas_call | solution.py:116
  (3 shorter events, 0.0 us)
Async XLA Ops:
  0.0 4.0 %copy-start.3 = (f32[16,256]{1,0:T(8,128)S(1)}, f32[16,256]{1,0:T(8,128)}, u32[]{:S(2)}) copy-start(f32[16,256]{1,0:T(8,128)} %param.2) | copy-start | bytes 49156
  0.0 4.0 %collective-permute-start = (f32[16,256]{1,0:T(8,128)}, f32[16,256]{1,0:T(8,128)S(1)}, u32[]{:S(2)}, u32[]{:S(2)}) collective-permute-start(f32[16,256]{1,0:T(8,128)} %param.2), channel_id=1, source_target_pairs={{0,1},{1,0},{2,3},{3,2},{4,5},{5,4},{6,7},{7,6},{8,9},{9,8},{10,11... | collective-permute-start | bytes 49160 | tf_op jit(solution)/shard_map/ppermute | solution.py:21
  4.0 5.8 %collective-permute-start.1 = (f32[16,512]{1,0:T(8,128)S(1)}, f32[16,512]{1,0:T(8,128)S(1)}, u32[]{:S(2)}, u32[]{:S(2)}) collective-permute-start(f32[16,512]{1,0:T(8,128)S(1)} %pad_maximum_fusion), channel_id=1, source_target_pairs={{0,2},{1,3},{2,0},{3,1},{4,6},{5,7},{6,4},{7,5},{8,10},{9,11},{10,... | collective-permute-start | bytes 98312 | tf_op jit(solution)/shard_map/ppermute | solution.py:21
  8.0 7.0 %copy-start.4 = (f32[16,255]{1,0:T(8,128)S(1)}, f32[16,255]{1,0:T(8,128)}, u32[]{:S(2)}) copy-start(f32[16,255]{1,0:T(8,128)} %param.3) | copy-start | bytes 48964
  9.8 7.0 %copy-start = (f32[16,1024]{1,0:T(8,128)}, f32[16,1024]{1,0:T(8,128)S(1)}, u32[]{:S(2)}) copy-start(f32[16,1024]{1,0:T(8,128)S(1)} %constant_dynamic-update-slice_fusion.row_ref) | copy-start | bytes 196612
  9.8 7.0 %collective-permute-start.3 = (f32[16,1024]{1,0:T(8,128)S(1)}, f32[16,1024]{1,0:T(8,128)S(1)}, u32[]{:S(2)}, u32[]{:S(2)}) collective-permute-start(f32[16,1024]{1,0:T(8,128)S(1)} %constant_dynamic-update-slice_fusion.row_ref), channel_id=1, source_target_pairs={{0,4},{1,5},{2,6},{3,7},{4,8},{5,9},{6,10},{7,11},{8,12},{9,13},{1... | collective-permute-start | bytes 196616 | tf_op jit(solution)/shard_map/ppermute | solution.py:21
  11.4 5.4 %collective-permute-start.2 = (f32[16,1024]{1,0:T(8,128)S(1)}, f32[16,1024]{1,0:T(8,128)S(1)}, u32[]{:S(2)}, u32[]{:S(2)}) collective-permute-start(f32[16,1024]{1,0:T(8,128)S(1)} %constant_dynamic-update-slice_fusion.row_ref), channel_id=1, source_target_pairs={{0,124},{1,125},{2,126},{3,127},{4,0},{5,1},{6,2},{7,3},{8,4},{9,5... | collective-permute-start | bytes 196616 | tf_op jit(solution)/shard_map/ppermute | solution.py:21
  16.9 0.6 %copy-start.1 = (f32[16,1024]{1,0:T(8,128)}, f32[16,1024]{1,0:T(8,128)S(1)}, u32[]{:S(2)}) copy-start(f32[16,1024]{1,0:T(8,128)S(1)} %collective-permute-done.3.before_ref) | copy-start | bytes 196612
  17.5 0.6 %copy-start.2 = (f32[16,1024]{1,0:T(8,128)}, f32[16,1024]{1,0:T(8,128)S(1)}, u32[]{:S(2)}) copy-start(f32[16,1024]{1,0:T(8,128)S(1)} %collective-permute-done.2.after_ref) | copy-start | bytes 196612
where the time goes:
time: 32.8 us; the launch traced here: 32.6 us
  Pallas kernels  14.5 us (44%)
  starting transfers between devices  11 us (34%)
  waiting for transfers between devices  4.47 us (14%)
  local copies, waits for them, and re-layouts  2.61 us (8%)
    pallas_call x1, Pallas kernels, shards(): pl.pallas_call(kernel, out_shape=jax.ShapeDtypeStruct((channels, BLOCK),...  14.5 us
    ppermute x4, starting transfers between devices, permute(): lax.ppermute(block, AXES, [(i, target(i) % count) for i in range(count)])  11 us
    ppermute x4, waiting for transfers between devices, permute(): lax.ppermute(block, AXES, [(i, target(i) % count) for i in range(count)])  4.47 us
    unnamed x12, local copies, waits for them, and re-layouts  2.01 us
  transfers between devices with their start and end apart: 4, of which 3 were waited for; matrix products, arithmetic and copies ran while one was open for 4% of the time, Pallas kernels for 0%

commit v1 on v0

v1 whole, which is shorter than its diff:
```python
import functools

import jax
import jax.numpy as jnp
from jax import lax
from jax.experimental import pallas as pl
from jax.experimental.pallas import tpu as pltpu
from jax.sharding import PartitionSpec as P

AXES = ("band", "col")
KD = 4
EPSILON = 1e-06
ROW = 4
BLOCK = 256
LANES = 128
HALO = KD - 1
SPAN = 2 * HALO + 1
UNROLL = 2
CHUNK = 32


def permute(block, target, count):
    return lax.ppermute(block, AXES, [(i, target(i) % count) for i in range(count)])


def kernel(row_ref, after_ref, before_ref, tail_ref, out_ref, line, wave, mean, scale, best_ref, *slots):
    channels = out_ref.shape[0]
    place = lax.axis_index("band") * lax.axis_size("col") + lax.axis_index("col")
    count = lax.axis_size("band") * lax.axis_size("col")
    here = lax.rem(place, ROW)

    for piece in range(ROW):
        at = (here ^ piece) * BLOCK
        source = slice(piece * BLOCK, (piece + 1) * BLOCK)
        for turn, ref in enumerate((before_ref, row_ref, after_ref)):
            target = pl.multiple_of(at + turn * ROW * BLOCK, BLOCK)
            line[:, pl.ds(target, BLOCK)] = ref[:, source]

    @pl.when(place + ROW >= count)
    def _():
        line[:, 2 * ROW * BLOCK : 2 * ROW * BLOCK + BLOCK - 1] = tail_ref[...]

    start = pl.multiple_of((here + ROW - HALO) * BLOCK, BLOCK)
    blocks = (SPAN + 1) * 2
    total = [line[:, pl.ds(pl.multiple_of(start + l * LANES, LANES), LANES)] for l in range(blocks)]
    for l in range(blocks):
        wave[l] = total[l]

    column = lax.broadcasted_iota(jnp.int32, (channels, LANES), 1)

    def shifted(values, by):
        if by == LANES:
            return values[1:] + values[-1:]
        turned = [pltpu.roll(v, LANES - by, 1) for v in values]
        inside = column < LANES - by
        return [jnp.where(inside, t, u) for t, u in zip(turned, turned[1:] + turned[-1:])]

    spread = None
    width = 1
    while width < BLOCK:
        other = shifted(total, width)
        gap = [o - t for o, t in zip(other, total)]
        gap = [g * g * (0.5 / width) for g in gap]
        if spread is None:
            spread = gap
        else:
            spread = [a + b + g for a, b, g in zip(spread, shifted(spread, width), gap)]
        total = [t + o for t, o in zip(total, other)]
        width *= 2
    for l in range(SPAN * 2):
        mean[l] = total[l] * (1.0 / BLOCK)
        scale[l] = lax.rsqrt(spread[l] * (1.0 / BLOCK) + EPSILON)

    behind = lax.broadcasted_iota(jnp.int32, (CHUNK, LANES), 1) - lax.broadcasted_iota(jnp.int32, (CHUNK, LANES), 0)

    def spanned(ref, c, l):
        row = ref[l, pl.ds(c, 8, stride=0), :]
        return jnp.broadcast_to(row[None], (CHUNK // 8, 8, LANES)).reshape(CHUNK, LANES)

    def windows(c, z_ref, own_ref, top_ref):
        for k in range(0, LANES, CHUNK):
            low = behind <= k

            def turned(l):
                return pltpu.roll(spanned(wave, c, l), k + 1, 1, stride=1, stride_axis=0)

            first, second = turned(0), turned(1)
            left = jnp.where(low, first, second)
            for l in range(SPAN * 2):
                third = turned(l + 2)
                right = jnp.where(low, second, third)
                a = spanned(mean, c, l)
                r = spanned(scale, c, l)
                z_ref[l, k : k + CHUNK] = ((left - a) * r).astype(jnp.bfloat16)
                z_ref[l, LANES + k : LANES + k + CHUNK] = ((right - a) * r).astype(jnp.bfloat16)
                left, second = right, third
            yield
        for l in range(2):
            own_ref[l] = z_ref[2 * HALO + l].T
        yield

    edge = BLOCK // 4

    def keep(score, offset):
        lag = lax.broadcasted_iota(jnp.int32, score.shape, 1) - lax.broadcasted_iota(jnp.int32, score.shape, 0)
        return jnp.where(jnp.abs(lag + offset) >= edge, score, -4.0 * BLOCK)

    def source(b):
        exists = (place + b - HALO >= 0) & (place + b - HALO < count)
        return jnp.where(exists, b, HALO + 2 if b < HALO else HALO - 2)

    sources = [HALO if b == HALO else source(b) for b in range(SPAN)]

    def tile(b, z_ref, own_ref, top_ref):
        at = 2 * sources[b]
        z = jnp.concatenate([z_ref[at], z_ref[at + 1]], axis=1)
        offset = b - HALO
        own = jnp.concatenate([own_ref[0], own_ref[1]], axis=0)
        score = jnp.dot(own, z, preferred_element_type=jnp.float32)
        left, rest = score[:, :LANES], score[:, LANES:]
        if offset == 0:
            left = jnp.concatenate([keep(left[: BLOCK - edge], 0), left[BLOCK - edge :]], axis=0)
            rest = jnp.concatenate([rest[:edge], keep(rest[edge:], LANES - edge)], axis=0)
        if offset == 1:
            left = jnp.concatenate([left[: BLOCK - edge], keep(left[BLOCK - edge :], edge)], axis=0)
        if offset == -1:
            rest = jnp.concatenate([keep(rest[:edge], LANES - BLOCK), rest[edge:]], axis=0)
        top = jnp.maximum(left, rest)
        top_ref[...] = jnp.maximum(top_ref[...], top) if b else top

    def finish(c, z_ref, own_ref, top_ref):
        best_ref[pl.ds(c, 1), :] = jnp.max(top_ref[...].T, axis=0, keepdims=True)

    first, second = slots[:3], slots[3:]

    def step(c, now, later):
        ahead = windows(jnp.minimum(c + 1, channels - 1), *later)
        finish(jnp.maximum(c - 1, 0), *later)
        parts = LANES // CHUNK + 1
        for b in range(SPAN):
            for _ in range(parts * b // (SPAN - 1), parts * (b + 1) // (SPAN - 1)):
                next(ahead, None)
            tile(b, *now)

    def several(k, carry):
        for u in range(UNROLL):
            now, later = (second, first) if u % 2 else (first, second)
            step(k * UNROLL + u, now, later)
        return carry

    for _ in windows(0, *first):
        pass
    lax.fori_loop(0, channels // UNROLL, several, 0)
    finish(channels - 1, *second)
    out_ref[...] = jnp.sqrt(2.0 * BLOCK - 2.0 * best_ref[...])


def shards(series, tail):
    channels = series.shape[0]
    count = lax.axis_size(AXES)
    pair = jnp.concatenate([series, permute(series, lambda i: i ^ 1, count)], axis=1)
    row = jnp.concatenate([pair, permute(pair, lambda i: i ^ 2, count)], axis=1)
    after = permute(row, lambda i: i - ROW, count)
    before = permute(row, lambda i: i + ROW, count)
    vmem = pl.BlockSpec(memory_space=pltpu.VMEM)
    return pl.pallas_call(
        kernel,
        out_shape=jax.ShapeDtypeStruct((channels, BLOCK), jnp.float32),
        in_specs=[vmem] * 4,
        out_specs=vmem,
        scratch_shapes=[
            pltpu.VMEM((channels, 3 * ROW * BLOCK), jnp.float32),
            pltpu.VMEM(((SPAN + 1) * 2, channels, LANES), jnp.float32),
            pltpu.VMEM((SPAN * 2, channels, LANES), jnp.float32),
            pltpu.VMEM((SPAN * 2, channels, LANES), jnp.float32),
            pltpu.VMEM((channels, BLOCK), jnp.float32),
        ]
        + [
            pltpu.VMEM((SPAN * 2, BLOCK, LANES), jnp.bfloat16),
            pltpu.VMEM((2, LANES, BLOCK), jnp.bfloat16),
            pltpu.VMEM((BLOCK, LANES), jnp.float32),
        ]
        * 2,
        compiler_params=pltpu.CompilerParams(vmem_limit_bytes=8 << 20),
    )(row, after, before, tail)


def solution(mesh):
    return jax.shard_map(
        shards,
        mesh=mesh,
        in_specs=(P(None, AXES), P()),
        out_specs=P(None, AXES),
        check_vma=False,
    )
```

time: 32.8 us -> 27.3 us (0.83)
  Pallas kernels: 14.5 us -> 10 us
  local copies, waits for them, and re-layouts: 2.61 us -> 0.77 us
  waiting for transfers between devices: 4.47 us -> 5.08 us
    pallas_call x1, Pallas kernels: 14.5 us -> 10 us  [shards(): pl.pallas_call(kernel, out_shape=jax.ShapeDtypeStruct((channels, BLOCK),...]
    unnamed x12 -> x6, local copies, waits for them, and re-layouts: 2.01 us -> 0.76 us
    ppermute x4, waiting for transfers between devices: 4.47 us -> 5.08 us  [permute(): lax.ppermute(block, AXES, [(i, target(i) % count) for i in range(count)])]
    pad x1 -> x0, local copies, waits for them, and re-layouts: 0.6 us -> none  [shards(): tail = jnp.pad(tail, ((0, 0), (0, 1)))]
  transfers between devices with their start and end apart: 4 -> 4, of which waited for: 3 -> 3; matrix products, arithmetic and copies ran while one was open for 4% -> 3% of each run, Pallas kernels for 0% -> 0%
where the time goes in v1:
time: 27.3 us; the launch traced here: 26.9 us
  starting transfers between devices  11 us (40%)
  Pallas kernels  10 us (37%)
  waiting for transfers between devices  5.08 us (19%)
  local copies, waits for them, and re-layouts  0.77 us (3%)
    ppermute x4, starting transfers between devices, permute(): lax.ppermute(block, AXES, [(i, target(i) % count) for i in range(count)])  11 us
    pallas_call x1, Pallas kernels, shards(): pl.pallas_call(kernel, out_shape=jax.ShapeDtypeStruct((channels, BLOCK),...  10 us
    ppermute x4, waiting for transfers between devices, permute(): lax.ppermute(block, AXES, [(i, target(i) % count) for i in range(count)])  5.08 us
    unnamed x6, local copies, waits for them, and re-layouts  0.76 us
  transfers between devices with their start and end apart: 4, of which 3 were waited for; matrix products, arithmetic and copies ran while one was open for 3% of the time, Pallas kernels for 0%

profile of v1, /device:TPU:0, one launch (start us, length us, event | category | flops | bytes accessed | tf_op | source)
XLA Modules:
  0.0 26.9 jit_solution(15797301646724789751)
XLA Ops:
  0.0 0.0 copy-start.1
  0.0 2.0 %collective-permute-start = (f32[16,256]{1,0:T(8,128)}, f32[16,256]{1,0:T(8,128)S(1)}, u32[]{:S(2)}, u32[]{:S(2)}) collective-permute-start(f32[16,256]{1,0:T(8,128)} %param.2), channel_id=1, source_target_pairs={{0,1},{1,0},{2,3},{3,2},{4,5},{5,4},{6,7},{7,6},{8,9},{9,8},{10,11... | collective-permute-start | bytes 49160 | tf_op jit(solution)/shard_map/ppermute | solution.py:23
  2.0 0.8 %constant_dynamic-update-slice_fusion.2 = f32[16,1024]{1,0:T(8,128)S(1)} fusion(f32[16,256]{1,0:T(8,128)} %param.2), kind=kLoop, calls=%fused_computation.3 | loop fusion | bytes 32768
  2.8 1.2 %collective-permute-done = f32[16,256]{1,0:T(8,128)S(1)} collective-permute-done((f32[16,256]{1,0:T(8,128)}, f32[16,256]{1,0:T(8,128)S(1)}, u32[]{:S(2)}, u32[]{:S(2)}) %collective-permute-start) | collective-permute-done | bytes 16416 | tf_op jit(solution)/shard_map/ppermute | solution.py:23
  4.0 0.0 copy-done.1
  4.0 3.9 %collective-permute-start.1 = (f32[16,512]{1,0:T(8,128)S(1)}, f32[16,512]{1,0:T(8,128)S(1)}, u32[]{:S(2)}, u32[]{:S(2)}) collective-permute-start(f32[16,512]{1,0:T(8,128)S(1)} %pad_maximum_fusion), channel_id=1, source_target_pairs={{0,2},{1,3},{2,0},{3,1},{4,6},{5,7},{6,4},{7,5},{8,10},{9,11},{10,... | collective-permute-start | bytes 98312 | tf_op jit(solution)/shard_map/ppermute | solution.py:23
  8.0 0.0 copy-start
  8.0 1.9 %collective-permute-done.1 = f32[16,512]{1,0:T(8,128)S(1)} collective-permute-done((f32[16,512]{1,0:T(8,128)S(1)}, f32[16,512]{1,0:T(8,128)S(1)}, u32[]{:S(2)}, u32[]{:S(2)}) %collective-permute-start.1) | collective-permute-done | bytes 32800 | tf_op jit(solution)/shard_map/ppermute | solution.py:23
  9.8 1.6 %collective-permute-start.3 = (f32[16,1024]{1,0:T(8,128)S(1)}, f32[16,1024]{1,0:T(8,128)S(1)}, u32[]{:S(2)}, u32[]{:S(2)}) collective-permute-start(f32[16,1024]{1,0:T(8,128)S(1)} %constant_dynamic-update-slice_fusion.row_ref), channel_id=1, source_target_pairs={{0,4},{1,5},{2,6},{3,7},{4,8},{5,9},{6,10},{7,11},{8,12},{9,13},{1... | collective-permute-start | bytes 196616 | tf_op jit(solution)/shard_map/ppermute | solution.py:23
  11.4 3.5 %collective-permute-start.2 = (f32[16,1024]{1,0:T(8,128)S(1)}, f32[16,1024]{1,0:T(8,128)S(1)}, u32[]{:S(2)}, u32[]{:S(2)}) collective-permute-start(f32[16,1024]{1,0:T(8,128)S(1)} %constant_dynamic-update-slice_fusion.row_ref), channel_id=1, source_target_pairs={{0,124},{1,125},{2,126},{3,127},{4,0},{5,1},{6,2},{7,3},{8,4},{9,5... | collective-permute-start | bytes 196616 | tf_op jit(solution)/shard_map/ppermute | solution.py:23
  14.9 1.9 %collective-permute-done.3.before_ref = f32[16,1024]{1,0:T(8,128)S(1)} collective-permute-done((f32[16,1024]{1,0:T(8,128)S(1)}, f32[16,1024]{1,0:T(8,128)S(1)}, u32[]{:S(2)}, u32[]{:S(2)}) %collective-permute-start.3) | collective-permute-done | bytes 65568 | tf_op jit(solution)/shard_map/ppermute | solution.py:23
  16.9 0.0 collective-permute-done.2.after_ref
  16.9 0.0 copy-done
  16.9 10.0 %shard_map.28 = f32[16,256]{1,0:T(8,128)} custom-call(f32[16,1024]{1,0:T(8,128)S(1)} %constant_dynamic-update-slice_fusion.row_ref, f32[16,1024]{1,0:T(8,128)S(1)} %collective-permute-done.2.after_ref, f32[16,1024]{1,0:T(8,128)S(1)} %collective-permute-done.3.before_ref, f32[16,255]{1,0:T(8,128)S(1)} %copy-done), custom_call_target="tpu_custom_call" | custom-call | tf_op jit(solution)/shard_map/pallas_call | solution.py:166
  (3 shorter events, 0.0 us)
Async XLA Ops:
  0.0 4.0 %copy-start.1 = (f32[16,256]{1,0:T(8,128)S(1)}, f32[16,256]{1,0:T(8,128)}, u32[]{:S(2)}) copy-start(f32[16,256]{1,0:T(8,128)} %param.2) | copy-start | bytes 49156
  0.0 4.0 %collective-permute-start = (f32[16,256]{1,0:T(8,128)}, f32[16,256]{1,0:T(8,128)S(1)}, u32[]{:S(2)}, u32[]{:S(2)}) collective-permute-start(f32[16,256]{1,0:T(8,128)} %param.2), channel_id=1, source_target_pairs={{0,1},{1,0},{2,3},{3,2},{4,5},{5,4},{6,7},{7,6},{8,9},{9,8},{10,11... | collective-permute-start | bytes 49160 | tf_op jit(solution)/shard_map/ppermute | solution.py:23
  4.0 5.8 %collective-permute-start.1 = (f32[16,512]{1,0:T(8,128)S(1)}, f32[16,512]{1,0:T(8,128)S(1)}, u32[]{:S(2)}, u32[]{:S(2)}) collective-permute-start(f32[16,512]{1,0:T(8,128)S(1)} %pad_maximum_fusion), channel_id=1, source_target_pairs={{0,2},{1,3},{2,0},{3,1},{4,6},{5,7},{6,4},{7,5},{8,10},{9,11},{10,... | collective-permute-start | bytes 98312 | tf_op jit(solution)/shard_map/ppermute | solution.py:23
  8.0 8.9 %copy-start = (f32[16,255]{1,0:T(8,128)S(1)}, f32[16,255]{1,0:T(8,128)}, u32[]{:S(2)}) copy-start(f32[16,255]{1,0:T(8,128)} %tail_ref.1) | copy-start | bytes 48964
  9.8 7.0 %collective-permute-start.3 = (f32[16,1024]{1,0:T(8,128)S(1)}, f32[16,1024]{1,0:T(8,128)S(1)}, u32[]{:S(2)}, u32[]{:S(2)}) collective-permute-start(f32[16,1024]{1,0:T(8,128)S(1)} %constant_dynamic-update-slice_fusion.row_ref), channel_id=1, source_target_pairs={{0,4},{1,5},{2,6},{3,7},{4,8},{5,9},{6,10},{7,11},{8,12},{9,13},{1... | collective-permute-start | bytes 196616 | tf_op jit(solution)/shard_map/ppermute | solution.py:23
  11.4 5.4 %collective-permute-start.2 = (f32[16,1024]{1,0:T(8,128)S(1)}, f32[16,1024]{1,0:T(8,128)S(1)}, u32[]{:S(2)}, u32[]{:S(2)}) collective-permute-start(f32[16,1024]{1,0:T(8,128)S(1)} %constant_dynamic-update-slice_fusion.row_ref), channel_id=1, source_target_pairs={{0,124},{1,125},{2,126},{3,127},{4,0},{5,1},{6,2},{7,3},{8,4},{9,5... | collective-permute-start | bytes 196616 | tf_op jit(solution)/shard_map/ppermute | solution.py:23

commit v2 on v1

--- a/solution.py
+++ b/solution.py
@@ -1,5 +1,3 @@
-import functools
-
 import jax
 import jax.numpy as jnp
 from jax import lax
@@ -7,10 +5,12 @@
 from jax.experimental.pallas import tpu as pltpu
 from jax.sharding import PartitionSpec as P
 
+
 AXES = ("band", "col")
 KD = 4
 EPSILON = 1e-06
 ROW = 4
+PAIR = ROW // 2
 BLOCK = 256
 LANES = 128
 HALO = KD - 1
@@ -23,18 +23,17 @@
     return lax.ppermute(block, AXES, [(i, target(i) % count) for i in range(count)])
 
 
-def kernel(row_ref, after_ref, before_ref, tail_ref, out_ref, line, wave, mean, scale, best_ref, *slots):
+def kernel(pair_ref, across_ref, first_ref, second_ref, third_ref, tail_ref, out_ref, line, wave, mean, scale, best_ref, *slots):
     channels = out_ref.shape[0]
     place = lax.axis_index("band") * lax.axis_size("col") + lax.axis_index("col")
     count = lax.axis_size("band") * lax.axis_size("col")
     here = lax.rem(place, ROW)
 
-    for piece in range(ROW):
-        at = (here ^ piece) * BLOCK
-        source = slice(piece * BLOCK, (piece + 1) * BLOCK)
-        for turn, ref in enumerate((before_ref, row_ref, after_ref)):
-            target = pl.multiple_of(at + turn * ROW * BLOCK, BLOCK)
-            line[:, pl.ds(target, BLOCK)] = ref[:, source]
+    late = here // PAIR
+    for ref, other, row in ((pair_ref, 0, 1), (across_ref, PAIR, 1), (first_ref, 0, 2 - 2 * late), (second_ref, 0, 2 * late), (third_ref, PAIR, 2 * late)):
+        for piece in range(PAIR):
+            target = pl.multiple_of(((here ^ (other + piece)) + ROW * row) * BLOCK, BLOCK)
+            line[:, pl.ds(target, BLOCK)] = ref[:, piece * BLOCK : (piece + 1) * BLOCK]
 
     @pl.when(place + ROW >= count)
     def _():
@@ -73,6 +72,8 @@
 
     behind = lax.broadcasted_iota(jnp.int32, (CHUNK, LANES), 1) - lax.broadcasted_iota(jnp.int32, (CHUNK, LANES), 0)
 
+    behind_own = lax.broadcasted_iota(jnp.int32, (LANES, LANES), 1) - lax.broadcasted_iota(jnp.int32, (LANES, LANES), 0)
+
     def spanned(ref, c, l):
         row = ref[l, pl.ds(c, 8, stride=0), :]
         return jnp.broadcast_to(row[None], (CHUNK // 8, 8, LANES)).reshape(CHUNK, LANES)
@@ -96,7 +97,8 @@
                 left, second = right, third
             yield
         for l in range(2):
-            own_ref[l] = z_ref[2 * HALO + l].T
+            turn = jnp.where(behind_own == 0, 1.0, 0.0).astype(jnp.bfloat16)
+            own_ref[l] = lax.dot_general(turn, z_ref[2 * HALO + l], (((1,), (1,)), ((), ())), preferred_element_type=jnp.float32).astype(jnp.bfloat16)
         yield
 
     edge = BLOCK // 4
@@ -129,18 +131,20 @@
         top_ref[...] = jnp.maximum(top_ref[...], top) if b else top
 
     def finish(c, z_ref, own_ref, top_ref):
-        best_ref[pl.ds(c, 1), :] = jnp.max(top_ref[...].T, axis=0, keepdims=True)
+        column = lax.broadcasted_iota(jnp.int32, (BLOCK, LANES), 1)
+        best_ref[...] = jnp.where(column == c, jnp.max(top_ref[...], axis=1, keepdims=True), best_ref[...])
 
     first, second = slots[:3], slots[3:]
 
     def step(c, now, later):
         ahead = windows(jnp.minimum(c + 1, channels - 1), *later)
-        finish(jnp.maximum(c - 1, 0), *later)
         parts = LANES // CHUNK + 1
         for b in range(SPAN):
             for _ in range(parts * b // (SPAN - 1), parts * (b + 1) // (SPAN - 1)):
                 next(ahead, None)
             tile(b, *now)
+            if b == 3:
+                finish(jnp.maximum(c - 1, 0), *later)
 
     def several(k, carry):
         for u in range(UNROLL):
@@ -152,28 +156,31 @@
         pass
     lax.fori_loop(0, channels // UNROLL, several, 0)
     finish(channels - 1, *second)
-    out_ref[...] = jnp.sqrt(2.0 * BLOCK - 2.0 * best_ref[...])
+    out_ref[...] = jnp.sqrt(2.0 * BLOCK - 2.0 * best_ref[...].T[:channels])
 
 
 def shards(series, tail):
     channels = series.shape[0]
     count = lax.axis_size(AXES)
+    forward = lambda i: i - ROW if i % ROW < PAIR else i + ROW
+    backward = lambda i: i + ROW if i % ROW < PAIR else i - ROW
     pair = jnp.concatenate([series, permute(series, lambda i: i ^ 1, count)], axis=1)
-    row = jnp.concatenate([pair, permute(pair, lambda i: i ^ 2, count)], axis=1)
-    after = permute(row, lambda i: i - ROW, count)
-    before = permute(row, lambda i: i + ROW, count)
+    first = permute(pair, forward, count)
+    across = permute(pair, lambda i: i ^ PAIR, count)
+    second = permute(pair, backward, count)
+    third = permute(first, lambda i: i ^ PAIR, count)
     vmem = pl.BlockSpec(memory_space=pltpu.VMEM)
     return pl.pallas_call(
         kernel,
         out_shape=jax.ShapeDtypeStruct((channels, BLOCK), jnp.float32),
-        in_specs=[vmem] * 4,
+        in_specs=[vmem] * 6,
         out_specs=vmem,
         scratch_shapes=[
             pltpu.VMEM((channels, 3 * ROW * BLOCK), jnp.float32),
             pltpu.VMEM(((SPAN + 1) * 2, channels, LANES), jnp.float32),
             pltpu.VMEM((SPAN * 2, channels, LANES), jnp.float32),
             pltpu.VMEM((SPAN * 2, channels, LANES), jnp.float32),
-            pltpu.VMEM((channels, BLOCK), jnp.float32),
+            pltpu.VMEM((BLOCK, LANES), jnp.float32),
         ]
         + [
             pltpu.VMEM((SPAN * 2, BLOCK, LANES), jnp.bfloat16),
@@ -182,7 +189,7 @@
         ]
         * 2,
         compiler_params=pltpu.CompilerParams(vmem_limit_bytes=8 << 20),
-    )(row, after, before, tail)
+    )(pair, across, first, second, third, tail)
 
 
 def solution(mesh):

time: 27.3 us -> 28.1 us (1.029)
  starting transfers between devices: 11 us -> 12.7 us
  Pallas kernels: 10 us -> 9.5 us
    ppermute x4 -> x5, starting transfers between devices: 11 us -> 12.7 us  [permute(): lax.ppermute(block, AXES, [(i, target(i) % count) for i in range(count)])]
    pallas_call x1, Pallas kernels: 10 us -> 9.5 us  [shards(): pl.pallas_call(kernel, out_shape=jax.ShapeDtypeStruct((channels, BLOCK),...]
    ppermute x4 -> x5, waiting for transfers between devices: 5.08 us -> 5 us  [permute(): lax.ppermute(block, AXES, [(i, target(i) % count) for i in range(count)])]
    unnamed x6 -> x3, local copies, waits for them, and re-layouts: 0.76 us -> 0.76 us
  transfers between devices with their start and end apart: 4 -> 5, of which waited for: 3 -> 3; matrix products, arithmetic and copies ran while one was open for 3% -> 3% of each run, Pallas kernels for 0% -> 0%
where the time goes in v2:
time: 28.1 us; the launch traced here: 27.9 us
  starting transfers between devices  12.7 us (45%)
  Pallas kernels  9.5 us (34%)
  waiting for transfers between devices  5 us (18%)
  local copies, waits for them, and re-layouts  0.76 us (3%)
    ppermute x5, starting transfers between devices, permute(): lax.ppermute(block, AXES, [(i, target(i) % count) for i in range(count)])  12.7 us
    pallas_call x1, Pallas kernels, shards(): pl.pallas_call(kernel, out_shape=jax.ShapeDtypeStruct((channels, BLOCK),...  9.5 us
    ppermute x5, waiting for transfers between devices, permute(): lax.ppermute(block, AXES, [(i, target(i) % count) for i in range(count)])  5 us
    unnamed x3, local copies, waits for them, and re-layouts  0.76 us
  transfers between devices with their start and end apart: 5, of which 3 were waited for; matrix products, arithmetic and copies ran while one was open for 3% of the time, Pallas kernels for 0%

profile of v2, /device:TPU:0, one launch (start us, length us, event | category | flops | bytes accessed | tf_op | source)
XLA Modules:
  0.0 27.9 jit_solution(17063666922800343574)
XLA Ops:
  0.0 2.0 %collective-permute-start = (f32[16,256]{1,0:T(8,128)}, f32[16,256]{1,0:T(8,128)S(1)}, u32[]{:S(2)}, u32[]{:S(2)}) collective-permute-start(f32[16,256]{1,0:T(8,128)} %param.2), channel_id=1, source_target_pairs={{0,1},{1,0},{2,3},{3,2},{4,5},{5,4},{6,7},{7,6},{8,9},{9,8},{10,11... | collective-permute-start | bytes 49160 | tf_op jit(solution)/shard_map/ppermute | solution.py:23
  2.0 0.8 %constant_dynamic-update-slice_fusion.1 = f32[16,512]{1,0:T(8,128)S(1)} fusion(f32[16,256]{1,0:T(8,128)} %param.2), kind=kLoop, calls=%fused_computation.1 | loop fusion | bytes 32768
  2.8 0.0 copy-start
  2.8 1.2 %collective-permute-done = f32[16,256]{1,0:T(8,128)S(1)} collective-permute-done((f32[16,256]{1,0:T(8,128)}, f32[16,256]{1,0:T(8,128)S(1)}, u32[]{:S(2)}, u32[]{:S(2)}) %collective-permute-start) | collective-permute-done | bytes 16416 | tf_op jit(solution)/shard_map/ppermute | solution.py:23
  4.0 3.8 %collective-permute-start.2 = (f32[16,512]{1,0:T(8,128)S(1)}, f32[16,512]{1,0:T(8,128)S(1)}, u32[]{:S(2)}, u32[]{:S(2)}) collective-permute-start(f32[16,512]{1,0:T(8,128)S(1)} %constant_dynamic-update-slice_fusion.pair_ref), channel_id=1, source_target_pairs={{0,124},{1,125},{2,6},{3,7},{4,0},{5,1},{6,10},{7,11},{8,4},{9,5},... | collective-permute-start | bytes 98312 | tf_op jit(solution)/shard_map/ppermute | solution.py:23
  7.7 0.0 collective-permute-start.3
  7.7 5.3 %collective-permute-start.1 = (f32[16,512]{1,0:T(8,128)S(1)}, f32[16,512]{1,0:T(8,128)S(1)}, u32[]{:S(2)}, u32[]{:S(2)}) collective-permute-start(f32[16,512]{1,0:T(8,128)S(1)} %constant_dynamic-update-slice_fusion.pair_ref), channel_id=1, source_target_pairs={{0,2},{1,3},{2,0},{3,1},{4,6},{5,7},{6,4},{7,5},{8,10},{9,11},{10,... | collective-permute-start | bytes 98312 | tf_op jit(solution)/shard_map/ppermute | solution.py:23
  13.0 0.0 collective-permute-done.2.first_ref
  13.0 1.6 %collective-permute-start.4 = (f32[16,512]{1,0:T(8,128)S(1)}, f32[16,512]{1,0:T(8,128)S(1)}, u32[]{:S(2)}, u32[]{:S(2)}) collective-permute-start(f32[16,512]{1,0:T(8,128)S(1)} %collective-permute-done.2.first_ref), channel_id=1, source_target_pairs={{0,2},{1,3},{2,0},{3,1},{4,6},{5,7},{6,4},{7,5},{8,10},{9,11},{10,... | collective-permute-start | bytes 98312 | tf_op jit(solution)/shard_map/ppermute | solution.py:23
  14.6 0.0 collective-permute-done.3.second_ref
  14.6 0.3 %collective-permute-done.1.across_ref = f32[16,512]{1,0:T(8,128)S(1)} collective-permute-done((f32[16,512]{1,0:T(8,128)S(1)}, f32[16,512]{1,0:T(8,128)S(1)}, u32[]{:S(2)}, u32[]{:S(2)}) %collective-permute-start.1) | collective-permute-done | bytes 32800 | tf_op jit(solution)/shard_map/ppermute | solution.py:23
  14.9 3.5 %collective-permute-done.4.third_ref = f32[16,512]{1,0:T(8,128)S(1)} collective-permute-done((f32[16,512]{1,0:T(8,128)S(1)}, f32[16,512]{1,0:T(8,128)S(1)}, u32[]{:S(2)}, u32[]{:S(2)}) %collective-permute-start.4) | collective-permute-done | bytes 32800 | tf_op jit(solution)/shard_map/ppermute | solution.py:23
  18.4 0.0 copy-done
  18.4 9.5 %shard_map.28 = f32[16,256]{1,0:T(8,128)} custom-call(f32[16,512]{1,0:T(8,128)S(1)} %constant_dynamic-update-slice_fusion.pair_ref, f32[16,512]{1,0:T(8,128)S(1)} %collective-permute-done.1.across_ref, f32[16,512]{1,0:T(8,128)S(1)} %collective-permute-done.2.first_ref, f32[16,512]{1,0:T(8,128)S(1)} %collective-permute-done.3.second_ref, ...), custom_call_target="tpu_custom_call" | custom-call | tf_op jit(solution)/shard_map/pallas_call | solution.py:173
  (1 shorter events, 0.0 us)
Async XLA Ops:
  0.0 4.0 %collective-permute-start = (f32[16,256]{1,0:T(8,128)}, f32[16,256]{1,0:T(8,128)S(1)}, u32[]{:S(2)}, u32[]{:S(2)}) collective-permute-start(f32[16,256]{1,0:T(8,128)} %param.2), channel_id=1, source_target_pairs={{0,1},{1,0},{2,3},{3,2},{4,5},{5,4},{6,7},{7,6},{8,9},{9,8},{10,11... | collective-permute-start | bytes 49160 | tf_op jit(solution)/shard_map/ppermute | solution.py:23
  2.8 15.7 %copy-start = (f32[16,255]{1,0:T(8,128)S(1)}, f32[16,255]{1,0:T(8,128)}, u32[]{:S(2)}) copy-start(f32[16,255]{1,0:T(8,128)} %tail_ref.1) | copy-start | bytes 48964
  4.0 9.1 %collective-permute-start.2 = (f32[16,512]{1,0:T(8,128)S(1)}, f32[16,512]{1,0:T(8,128)S(1)}, u32[]{:S(2)}, u32[]{:S(2)}) collective-permute-start(f32[16,512]{1,0:T(8,128)S(1)} %constant_dynamic-update-slice_fusion.pair_ref), channel_id=1, source_target_pairs={{0,124},{1,125},{2,6},{3,7},{4,0},{5,1},{6,10},{7,11},{8,4},{9,5},... | collective-permute-start | bytes 98312 | tf_op jit(solution)/shard_map/ppermute | solution.py:23
  7.7 6.9 %collective-permute-start.3 = (f32[16,512]{1,0:T(8,128)S(1)}, f32[16,512]{1,0:T(8,128)S(1)}, u32[]{:S(2)}, u32[]{:S(2)}) collective-permute-start(f32[16,512]{1,0:T(8,128)S(1)} %constant_dynamic-update-slice_fusion.pair_ref), channel_id=1, source_target_pairs={{0,4},{1,5},{2,126},{3,127},{4,8},{5,9},{6,2},{7,3},{8,12},{9,13},... | collective-permute-start | bytes 98312 | tf_op jit(solution)/shard_map/ppermute | solution.py:23
  7.7 7.2 %collective-permute-start.1 = (f32[16,512]{1,0:T(8,128)S(1)}, f32[16,512]{1,0:T(8,128)S(1)}, u32[]{:S(2)}, u32[]{:S(2)}) collective-permute-start(f32[16,512]{1,0:T(8,128)S(1)} %constant_dynamic-update-slice_fusion.pair_ref), channel_id=1, source_target_pairs={{0,2},{1,3},{2,0},{3,1},{4,6},{5,7},{6,4},{7,5},{8,10},{9,11},{10,... | collective-permute-start | bytes 98312 | tf_op jit(solution)/shard_map/ppermute | solution.py:23
  13.0 5.4 %collective-permute-start.4 = (f32[16,512]{1,0:T(8,128)S(1)}, f32[16,512]{1,0:T(8,128)S(1)}, u32[]{:S(2)}, u32[]{:S(2)}) collective-permute-start(f32[16,512]{1,0:T(8,128)S(1)} %collective-permute-done.2.first_ref), channel_id=1, source_target_pairs={{0,2},{1,3},{2,0},{3,1},{4,6},{5,7},{6,4},{7,5},{8,10},{9,11},{10,... | collective-permute-start | bytes 98312 | tf_op jit(solution)/shard_map/ppermute | solution.py:23
